TPU v7x, 32 devices: a whole 2x2x4 slice. The times are simulated.
32 devices in a mesh: expert: 4 (over z), tensor: 8 (over y, x, core).
Axes of the slice: x: 2, y: 2, z: 4, core: 2. Of those that a mesh axis runs over, the one named last changes fastest.
Arguments:
- tokens: bfloat16 [512, 6144], P('expert', 'tensor'), may hold values from -6 to 6
- out_grad: bfloat16 [512, 6144], P('expert', 'tensor'), may hold values from -6 to 6
- expert_ids: int32 [512, 2], P('expert'), may hold values from 0 to 3, all different within a row; in each aligned block of 128 rows (0 to 127, 128 to 255, ...) at most 80 rows name the same one
- route_logits: float32 [512, 2], P('expert'), may hold values from -6 to 6
- w_gate: bfloat16 [4, 6144, 8192], P('expert', 'tensor'), may hold values from -0.078125 to 0.078125
- w_up: bfloat16 [4, 6144, 8192], P('expert', 'tensor'), may hold values from -0.078125 to 0.078125
- w_down: bfloat16 [4, 6144, 8192], P('expert', 'tensor'), may hold values from -0.0625 to 0.0625
- gate_scale: float32 [4, 8192], P('expert', 'tensor'), may hold values from 0.5 to 2
- up_scale: float32 [4, 8192], P('expert', 'tensor'), may hold values from 0.5 to 2
- down_scale: float32 [4, 8192], P('expert', 'tensor'), may hold values from 0.5 to 2
Outputs:
- mixed: bfloat16 [512, 6144], P('expert', 'tensor')
- token_grad: bfloat16 [512, 6144], P('expert', 'tensor')
- logit_grad: float32 [512, 2], P('expert')
- gate_grad: bfloat16 [4, 6144, 8192], P('expert', None, 'tensor')
- up_grad: bfloat16 [4, 6144, 8192], P('expert', None, 'tensor')
- down_grad: bfloat16 [4, 6144, 8192], P('expert', None, 'tensor')
Inputs may be any that keep to these rules, and one draw needn't show every extreme that they name: `expert_ids`: each token names two different experts; among the 128 tokens of one index of the expert axis, each expert is named by at most 80.
All inputs are finite; a program needn't handle non-finite values.
Results may differ from a plain program's by a relative error of at most 0.025.
Values may be sent and summed in bfloat16 or wider, within the bound.
A program may use at most 256 MiB of HBM per device.

v0:
```python
import jax
import jax.numpy as jnp
from jax import lax
from jax.sharding import PartitionSpec as P


def gate_tables(expert_ids, route_logits, count):
    first = jax.nn.sigmoid(route_logits[:, 0] - route_logits[:, 1])
    probs = jnp.stack([first, 1.0 - first], axis=1)
    labels = jnp.arange(count, dtype=jnp.int32)
    chosen = (expert_ids[:, :, None] == labels[None, None, :]).astype(jnp.float32)
    per_expert = jnp.sum(probs[:, :, None] * chosen, axis=1)
    member = jnp.sum(chosen, axis=1)
    return (probs, chosen, per_expert, member)


def contract_rows(left, right):
    return lax.dot_general(
        left, right, (((0,), (0,)), ((), ())), preferred_element_type=jnp.float32
    )


def body(
    tokens,
    out_grad,
    expert_ids,
    route_logits,
    w_gate,
    w_up,
    w_down,
    gate_scale,
    up_scale,
    down_scale,
):
    groups = lax.axis_size("expert")
    local_tokens, feat_width = tokens.shape
    probs, chosen, per_expert, member = gate_tables(expert_ids, route_logits, groups)
    member_cols = member.T.astype(jnp.bfloat16)[:, :, None]
    weight_cols = per_expert.T[:, :, None]

    def unpacking(packed):
        return packed.astype(jnp.float32)

    total_rows = groups * local_tokens
    send_rows = tokens[None] * member_cols
    send_grads = (out_grad.astype(jnp.float32)[None] * weight_cols).astype(jnp.bfloat16)
    got_rows, got_grads = (
        lax.all_to_all(send_rows, "expert", split_axis=0, concat_axis=0, tiled=True),
        lax.all_to_all(send_grads, "expert", split_axis=0, concat_axis=0, tiled=True),
    )
    rows_in, grads_in = (
        lax.all_gather(got_rows.reshape(total_rows, feat_width), "tensor", axis=1, tiled=True),
        lax.all_gather(got_grads.reshape(total_rows, feat_width), "tensor", axis=1, tiled=True),
    )
    gate_all, up_all, down_all = (
        lax.all_to_all(w_gate, "tensor", split_axis=2, concat_axis=1, tiled=True),
        lax.all_to_all(w_up, "tensor", split_axis=2, concat_axis=1, tiled=True),
        lax.all_to_all(w_down, "tensor", split_axis=2, concat_axis=1, tiled=True),
    )
    gate_w = gate_all[0]
    up_w = up_all[0]
    down_w = down_all[0]
    gate_pre = jnp.dot(rows_in, gate_w, preferred_element_type=jnp.float32) * gate_scale[0]
    up_pre = jnp.dot(rows_in, up_w, preferred_element_type=jnp.float32) * up_scale[0]
    sigma = jax.nn.sigmoid(gate_pre)
    active = gate_pre * sigma
    hidden = (active * up_pre * down_scale[0]).astype(jnp.bfloat16)
    out_part = jnp.dot(hidden, down_w.T, preferred_element_type=jnp.float32)
    down_grad = contract_rows(grads_in, hidden).astype(jnp.bfloat16)
    back = jnp.dot(grads_in, down_w, preferred_element_type=jnp.float32) * down_scale[0]
    d_gate = (back * up_pre * sigma * (1.0 + gate_pre * (1.0 - sigma)) * gate_scale[0]).astype(
        jnp.bfloat16
    )
    d_up = (back * active * up_scale[0]).astype(jnp.bfloat16)
    gate_grad = contract_rows(rows_in, d_gate).astype(jnp.bfloat16)
    up_grad = contract_rows(rows_in, d_up).astype(jnp.bfloat16)
    grad_part = jnp.dot(d_gate, gate_w.T, preferred_element_type=jnp.float32) + jnp.dot(
        d_up, up_w.T, preferred_element_type=jnp.float32
    )
    out_sum = lax.psum_scatter(
        out_part.astype(jnp.bfloat16), "tensor", scatter_dimension=1, tiled=True
    )
    out_back = lax.all_to_all(
        out_sum.reshape(groups, local_tokens, feat_width),
        "expert",
        split_axis=0,
        concat_axis=0,
        tiled=True,
    )
    grad_sum = lax.psum_scatter(
        grad_part.astype(jnp.bfloat16), "tensor", scatter_dimension=1, tiled=True
    )
    grad_back = lax.all_to_all(
        grad_sum.reshape(groups, local_tokens, feat_width),
        "expert",
        split_axis=0,
        concat_axis=0,
        tiled=True,
    )
    out_float = unpacking(out_back)
    grad_float = unpacking(grad_back)
    mixed = jnp.sum(weight_cols * out_float, axis=0).astype(jnp.bfloat16)
    token_grad = jnp.sum(grad_float, axis=0).astype(jnp.bfloat16)
    local_score = jnp.einsum("td,etd->te", out_grad.astype(jnp.float32), out_float)
    score = lax.psum(local_score, "tensor")
    pick = jnp.sum(chosen * score[:, None, :], axis=2)
    mean_pick = jnp.sum(probs * pick, axis=1, keepdims=True)
    logit_grad = probs * (pick - mean_pick)
    return (mixed, token_grad, logit_grad, gate_grad[None], up_grad[None], down_grad[None])


def solution(mesh):
    in_specs = (
        P("expert", "tensor"),
        P("expert", "tensor"),
        P("expert", None),
        P("expert", None),
        P("expert", "tensor", None),
        P("expert", "tensor", None),
        P("expert", "tensor", None),
        P("expert", "tensor"),
        P("expert", "tensor"),
        P("expert", "tensor"),
    )
    out_specs = (
        P("expert", "tensor"),
        P("expert", "tensor"),
        P("expert", None),
        P("expert", None, "tensor"),
        P("expert", None, "tensor"),
        P("expert", None, "tensor"),
    )
    return jax.shard_map(body, mesh=mesh, in_specs=in_specs, out_specs=out_specs, check_vma=False)
```

profile of v0, /device:TPU:0, one launch (start us, length us, event | category | flops | bytes accessed | tf_op | source)
XLA Modules:
  0.0 1169.5 jit_solution(9757918283287078089)
XLA Ops:
  16.1 51.2 %copy.36 = bf16[1,768,8192]{1,0,2:T(2,128)(2,1)} copy(bf16[1,768,8192]{2,1,0:T(8,128)(2,1)} %param.14) | data formatting | bytes 25165824 | tf_op args[4]
  67.9 126.8 %reduce.1 = bf16[8192,768]{1,0:T(8,128)(2,1)} reduce(bf16[8192,1,768]{2,1,0:T(2,128)(2,1)} %bitcast.55, bf16[]{:T(256)} %broadcast.37), dimensions={1}, to_apply=%bitcast.33.reduce_sub_computation | reduce | bytes 25165826
  213.4 51.2 %copy.38 = bf16[1,768,8192]{1,0,2:T(2,128)(2,1)} copy(bf16[1,768,8192]{2,1,0:T(8,128)(2,1)} %param.15) | data formatting | bytes 25165824 | tf_op args[5]
  264.7 126.8 %reduce.2 = bf16[8192,768]{1,0:T(8,128)(2,1)} reduce(bf16[8192,1,768]{2,1,0:T(2,128)(2,1)} %bitcast.60, bf16[]{:T(256)} %broadcast.37), dimensions={1}, to_apply=%bitcast.31.reduce_sub_computation | reduce | bytes 25165826
  409.3 51.2 %copy.40 = bf16[1,768,8192]{1,0,2:T(2,128)(2,1)} copy(bf16[1,768,8192]{2,1,0:T(8,128)(2,1)} %param.16) | data formatting | bytes 25165824 | tf_op args[6]
  460.5 126.8 %reduce.3 = bf16[8192,768]{1,0:T(8,128)(2,1)} reduce(bf16[8192,1,768]{2,1,0:T(2,128)(2,1)} %bitcast.56, bf16[]{:T(256)} %broadcast.37), dimensions={1}, to_apply=%bitcast.35.reduce_sub_computation | reduce | bytes 25165826
  606.0 18.0 %reshape.44 = bf16[8192,1,768]{2,1,0:T(2,128)(2,1)} reshape(bf16[8,2,393216]{2,1,0:T(2,128)(2,1)} %all-to-all-done.1) | data formatting | bytes 25165824
  623.9 15.1 %copy.45 = bf16[1,768,8192]{1,2,0:T(8,128)(2,1)} copy(bf16[1,768,8192]{1,0,2:T(2,128)(2,1)} %bitcast.57) | data formatting | bytes 25165824
  639.0 16.6 %copy.37 = bf16[1,8,768,1024]{3,2,1,0:T(8,128)(2,1)} copy(bf16[1,8,768,1024]{2,3,1,0:T(8,128)(2,1)} %bitcast.61) | data formatting | bytes 25165824 | tf_op jit(solution)/shard_map/all_to_all | solution.py:56
  655.6 18.1 %reshape.42 = bf16[8192,1,768]{2,1,0:T(2,128)(2,1)} reshape(bf16[8,2,393216]{2,1,0:T(2,128)(2,1)} %all-to-all-done.2) | data formatting | bytes 25165824
  673.7 15.1 %copy.46 = bf16[1,768,8192]{1,2,0:T(8,128)(2,1)} copy(bf16[1,768,8192]{1,0,2:T(2,128)(2,1)} %bitcast.58) | data formatting | bytes 25165824
  688.7 16.6 %copy.39 = bf16[1,8,768,1024]{3,2,1,0:T(8,128)(2,1)} copy(bf16[1,8,768,1024]{2,3,1,0:T(8,128)(2,1)} %bitcast.62) | data formatting | bytes 25165824 | tf_op jit(solution)/shard_map/all_to_all | solution.py:57
  705.3 63.9 %all-to-all-done.3 = bf16[8,2,393216]{2,1,0:T(2,128)(2,1)} async-done(((bf16[8,2,393216]{2,1,0:T(2,128)(2,1)}), bf16[8,2,393216]{2,1,0:T(2,128)(2,1)}, u32[]{:S(2)}, u32[]{:S(2)}) %all-to-all-start.3) | async-done | bytes 12582944 | tf_op jit(solution)/shard_map/all_to_all | solution.py:58
  769.2 17.9 %reshape.46 = bf16[8192,1,768]{2,1,0:T(2,128)(2,1)} reshape(bf16[8,2,393216]{2,1,0:T(2,128)(2,1)} %all-to-all-done.3) | data formatting | bytes 25165824
  787.1 15.1 %copy.47 = bf16[1,768,8192]{1,2,0:T(8,128)(2,1)} copy(bf16[1,768,8192]{1,0,2:T(2,128)(2,1)} %bitcast.59) | data formatting | bytes 25165824
  802.2 16.6 %copy.41 = bf16[1,8,768,1024]{3,2,1,0:T(8,128)(2,1)} copy(bf16[1,8,768,1024]{2,3,1,0:T(8,128)(2,1)} %bitcast.63) | data formatting | bytes 25165824 | tf_op jit(solution)/shard_map/all_to_all | solution.py:58
  853.9 61.4 %reduce-scatter.3.cloned.1.call-done = bf16[512,768]{1,0:T(8,128)(2,1)} async-done(((bf16[512,6144]{1,0:T(8,128)(2,1)}), bf16[512,768]{1,0:T(8,128)(2,1)}) %reduce-scatter.3.cloned.1.call-update) | async-done | bytes 786448 | tf_op jit(solution)/shard_map/reduce_scatter | solution.py:80
  920.0 19.9 %all-to-all-done.4 = bf16[4,128,768]{2,1,0:T(8,128)(2,1)S(1)} async-done(((bf16[4,128,768]{2,1,0:T(8,128)(2,1)}), bf16[4,128,768]{2,1,0:T(8,128)(2,1)S(1)}, u32[]{:S(2)}, u32[]{:S(2)}) %all-to-all-start.4) | async-done | bytes 786464 | tf_op jit(solution)/shard_map/all_to_all | solution.py:83
  953.9 23.3 %all_to_all.65 = bf16[4,128,768]{2,1,0:T(8,128)(2,1)} all-to-all(bf16[4,128,768]{2,1,0:T(8,128)(2,1)S(1)} %get-tuple-element.12), channel_id=1, replica_groups=mesh['expert'=4,'tensor'=8] {'expert'}, dimensions={0} | all-to-all | bytes 1572864 | tf_op jit(solution)/shard_map/all_to_all | solution.py:49
  977.3 43.5 %all-gather.5.cloned.1.call-done = bf16[512,6144]{1,0:T(8,128)(2,1)} async-done(((bf16[512,768]{1,0:T(8,128)(2,1)}), bf16[512,6144]{1,0:T(8,128)(2,1)}) %all-gather.5.cloned.1.call-update) | async-done | bytes 6291472 | tf_op jit(solution)/shard_map/all_gather | solution.py:53
  1020.8 14.3 %multiply_convert_fusion = (bf16[512,1024]{1,0:T(8,128)(2,1)S(1)}, bf16[512,1024]{1,0:T(8,128)(2,1)S(1)}) fusion(f32[1024]{0:T(1024)S(1)} %bitcast.83, f32[1024]{0:T(1024)S(1)} %bitcast.85, f32[512,1024]{1,0:T(8,128)} %copy-done.12, f32[1024]{0:T(1024)S(1)} %bitcast.87, f32[512,1024]{1,0:T(8,128)} %get-tuple-element.15, ...), kind=kOutput, calls=%fused_computation.5 | convolution fusion | flops 6451888128 | bytes 25178112 | tf_op jit(solution)/shard_map/dot_general | solution.py:70
  1035.1 20.2 %fusion.5 = f32[512,6144]{1,0:T(8,128)} fusion(bf16[512,1024]{1,0:T(8,128)(2,1)S(1)} %get-tuple-element.11, bf16[6144,1024]{1,0:T(8,128)(2,1)} %bitcast.65), kind=kOutput, calls=%fused_computation.27 | convolution fusion | flops 6442450944 | bytes 26214400 | tf_op jit(solution)/shard_map/dot_general | solution.py:77
  1055.4 20.3 %add_convert_fusion = bf16[512,6144]{1,0:T(8,128)(2,1)} fusion(f32[512,6144]{1,0:T(8,128)} %fusion.5, bf16[512,1024]{1,0:T(8,128)(2,1)S(1)} %get-tuple-element.10, bf16[6144,1024]{1,0:T(8,128)(2,1)} %bitcast.67), kind=kOutput, calls=%fused_computation.3 | convolution fusion | flops 6448742400 | bytes 32505856 | tf_op jit(solution)/shard_map/dot_general | solution.py:77
  1098.7 38.8 %reduce-scatter.5.cloned.1.call-done = bf16[512,768]{1,0:T(8,128)(2,1)} async-done(((bf16[512,6144]{1,0:T(8,128)(2,1)}), bf16[512,768]{1,0:T(8,128)(2,1)}) %reduce-scatter.5.cloned.1.call-update) | async-done | bytes 786448 | tf_op jit(solution)/shard_map/reduce_scatter | solution.py:90
  (80 shorter events, 166.8 us)
Async XLA Ops:
  9.8 197.2 %all-to-all-start = ((bf16[4,128,768]{2,1,0:T(8,128)(2,1)}), bf16[4,128,768]{2,1,0:T(8,128)(2,1)S(1)}, u32[]{:S(2)}, u32[]{:S(2)}) async-start(bf16[4,128,768]{2,1,0:T(8,128)(2,1)} %broadcast_multiply_fusion), calls=%async_computation | async-start | bytes 1572864 | tf_op jit(solution)/shard_map/all_to_all | solution.py:48
  207.9 195.9 %all-to-all-start.1 = ((bf16[8,2,393216]{2,1,0:T(2,128)(2,1)}), bf16[8,2,393216]{2,1,0:T(2,128)(2,1)}, u32[]{:S(2)}, u32[]{:S(2)}) async-start(bf16[8,2,393216]{2,1,0:T(2,128)(2,1)} %reshape.43), calls=%async_computation.1 | async-start | bytes 25165824 | tf_op jit(solution)/shard_map/all_to_all | solution.py:56
  403.7 195.9 %all-to-all-start.2 = ((bf16[8,2,393216]{2,1,0:T(2,128)(2,1)}), bf16[8,2,393216]{2,1,0:T(2,128)(2,1)}, u32[]{:S(2)}, u32[]{:S(2)}) async-start(bf16[8,2,393216]{2,1,0:T(2,128)(2,1)} %reshape.41), calls=%async_computation.2 | async-start | bytes 25165824 | tf_op jit(solution)/shard_map/all_to_all | solution.py:57
  599.6 169.6 %all-to-all-start.3 = ((bf16[8,2,393216]{2,1,0:T(2,128)(2,1)}), bf16[8,2,393216]{2,1,0:T(2,128)(2,1)}, u32[]{:S(2)}, u32[]{:S(2)}) async-start(bf16[8,2,393216]{2,1,0:T(2,128)(2,1)} %reshape.45), calls=%async_computation.3 | async-start | bytes 25165824 | tf_op jit(solution)/shard_map/all_to_all | solution.py:58
  604.9 213.9 %all-gather.3.cloned.1.call-start = ((), (), s32[]{:S(2)}) async-start(), calls=%async_computation.9 | async-start | bytes 7077888 | tf_op jit(solution)/shard_map/all_gather | solution.py:52
  605.7 309.6 %reduce-scatter.3.cloned.1.call-start = ((), (), s32[]{:S(2)}) async-start(), calls=%async_computation.10 | async-start | bytes 7077888 | tf_op jit(solution)/shard_map/reduce_scatter | solution.py:80
  818.8 13.6 %copy-start.4 = (bf16[512,6144]{1,0:T(8,128)(2,1)S(1)}, bf16[512,6144]{1,0:T(8,128)(2,1)}, u32[]{:S(2)}) copy-start(bf16[512,6144]{1,0:T(8,128)(2,1)} %all-gather.3.cloned.1.call-done) | copy-start | bytes 18874372
  818.8 13.6 %copy-start.5 = (f32[1,1024]{1,0:T(1,128)S(1)}, f32[1,1024]{1,0:T(1,128)}, u32[]{:S(2)}) copy-start(f32[1,1024]{1,0:T(1,128)} %param.19) | copy-start | bytes 12292
  818.8 13.6 %copy-start.6 = (f32[1,1024]{1,0:T(1,128)S(1)}, f32[1,1024]{1,0:T(1,128)}, u32[]{:S(2)}) copy-start(f32[1,1024]{1,0:T(1,128)} %param.18) | copy-start | bytes 12292
  818.9 13.6 %copy-start.7 = (f32[1,1024]{1,0:T(1,128)S(1)}, f32[1,1024]{1,0:T(1,128)}, u32[]{:S(2)}) copy-start(f32[1,1024]{1,0:T(1,128)} %param.17) | copy-start | bytes 12292
  818.9 26.4 %slice-start = ((s8[12582912]{0:T(1024)(128)(4,1)}), s8[4194304]{0:T(1024)(128)(4,1)S(1)}, s32[]{:S(2)}) async-start(s8[12582912]{0:T(1024)(128)(4,1)} %bitcast.69), calls=%async_computation.13 | async-start | bytes 8388608
  818.9 26.4 %slice-start.1 = ((s8[12582912]{0:T(1024)(128)(4,1)}), s8[4194304]{0:T(1024)(128)(4,1)S(1)}, s32[]{:S(2)}) async-start(s8[12582912]{0:T(1024)(128)(4,1)} %bitcast.69), calls=%async_computation.14 | async-start | bytes 8388608
  832.5 12.8 %slice-start.2 = ((s8[12582912]{0:T(1024)(128)(4,1)}), s8[4194304]{0:T(1024)(128)(4,1)S(1)}, s32[]{:S(2)}) async-start(s8[12582912]{0:T(1024)(128)(4,1)} %bitcast.69), calls=%async_computation.15 | async-start | bytes 8388608
  853.9 66.0 %copy-start.1 = (bf16[128,768]{1,0:T(8,128)(2,1)S(1)}, bf16[128,768]{1,0:T(8,128)(2,1)}, u32[]{:S(2)}) copy-start(bf16[128,768]{1,0:T(8,128)(2,1)} %param.11) | copy-start | bytes 589828
  853.9 66.0 %copy-start.3 = (f32[128,2]{0,1:T(2,128)S(1)}, f32[128,2]{0,1:T(2,128)}, u32[]{:S(2)}) copy-start(f32[128,2]{0,1:T(2,128)} %param.13) | copy-start | bytes 3076
  853.9 99.0 %copy-start.2 = (s32[128,2]{0,1:T(2,128)S(1)}, s32[128,2]{0,1:T(2,128)}, u32[]{:S(2)}) copy-start(s32[128,2]{0,1:T(2,128)} %param.12) | copy-start | bytes 3076
  915.3 24.5 %all-to-all-start.4 = ((bf16[4,128,768]{2,1,0:T(8,128)(2,1)}), bf16[4,128,768]{2,1,0:T(8,128)(2,1)S(1)}, u32[]{:S(2)}, u32[]{:S(2)}) async-start(bf16[4,128,768]{2,1,0:T(8,128)(2,1)} %bitcast.75), calls=%async_computation.5 | async-start | bytes 1572864 | tf_op jit(solution)/shard_map/all_to_all | solution.py:83
  919.9 100.9 %all-gather.5.cloned.1.call-start = ((), (), s32[]{:S(2)}) async-start(), calls=%async_computation.11 | async-start | bytes 7077888 | tf_op jit(solution)/shard_map/all_gather | solution.py:53
  977.3 160.1 %reduce-scatter.5.cloned.1.call-start = ((), (), s32[]{:S(2)}) async-start(), calls=%async_computation.12 | async-start | bytes 7077888 | tf_op jit(solution)/shard_map/reduce_scatter | solution.py:90
  1035.1 20.2 %copy-start.8 = (bf16[512,1024]{1,0:T(8,128)(2,1)}, bf16[512,1024]{1,0:T(8,128)(2,1)S(1)}, u32[]{:S(2)}) copy-start(bf16[512,1024]{1,0:T(8,128)(2,1)S(1)} %get-tuple-element.11) | copy-start | bytes 3145732
  1035.1 20.2 %copy-start.11 = (bf16[512,1024]{1,0:T(8,128)(2,1)}, bf16[512,1024]{1,0:T(8,128)(2,1)S(1)}, u32[]{:S(2)}) copy-start(bf16[512,1024]{1,0:T(8,128)(2,1)S(1)} %get-tuple-element.10) | copy-start | bytes 3145732
  1075.6 13.2 %slice-start.3 = ((s8[6291456]{0:T(1024)(128)(4,1)}), s8[2097152]{0:T(1024)(128)(4,1)S(1)}, s32[]{:S(2)}) async-start(s8[6291456]{0:T(1024)(128)(4,1)} %bitcast.80), calls=%async_computation.16 | async-start | bytes 4194304
  1076.2 12.6 %copy-start.9 = (bf16[512,1024]{1,0:T(8,128)(2,1)S(1)}, bf16[512,1024]{1,0:T(8,128)(2,1)}, u32[]{:S(2)}) copy-start(bf16[512,1024]{1,0:T(8,128)(2,1)} %copy-done.8) | copy-start | bytes 3145732
  1137.4 24.5 %all-to-all-start.6 = ((bf16[4,128,768]{2,1,0:T(8,128)(2,1)}), bf16[4,128,768]{2,1,0:T(8,128)(2,1)S(1)}, u32[]{:S(2)}, u32[]{:S(2)}) async-start(bf16[4,128,768]{2,1,0:T(8,128)(2,1)} %bitcast.74), calls=%async_computation.8 | async-start | bytes 1572864 | tf_op jit(solution)/shard_map/all_to_all | solution.py:93
  (4 other events, 26.3 us)
Sparse Core Ops, SparseCore 0:
  607.6 112.5 all-gather.2
  854.0 61.2 reduce-scatter.2
  977.4 43.3 all-gather.4
  1075.8 61.6 reduce-scatter.4
where the time goes:
time: 1180 us; the launch traced here: 1170 us
  other arithmetic  385 us (33%)
  local copies, waits for them, and re-layouts  342 us (29%)
  waiting for transfers between devices  236 us (20%)
  matrix products  124 us (11%)
  blocking collectives  35.3 us (3%)
  starting transfers between devices  32.3 us (3%)
  between operations  14.2 us (1%)
    unnamed x5, other arithmetic  380 us
    unnamed x49, local copies, waits for them, and re-layouts  292 us
    all_to_all x1, waiting for transfers between devices, body(): lax.all_to_all(w_down, 'tensor', split_axis=2, concat_axis=1, tiled=True)  63.9 us
    reduce_scatter x1, waiting for transfers between devices, body(): lax.psum_scatter(out_part.astype(jnp.bfloat16), 'tensor', scatter_dimensi...  61.4 us
    all_gather x1, waiting for transfers between devices, body(): lax.all_gather(got_grads.reshape(total_rows, feat_width), 'tensor', axis=...  43.5 us
    reduce_scatter x1, waiting for transfers between devices, body(): lax.psum_scatter(grad_part.astype(jnp.bfloat16), 'tensor', scatter_dimens...  38.8 us
    dot_general x3, matrix products, contract_rows(): lax.dot_general(left, right, (((0,), (0,)), ((), ())), preferred_element_...  34.2 us
  transfers between devices with their start and end apart: 10, of which 6 were waited for; matrix products, arithmetic and copies ran while one was open for 65% of the time, Pallas kernels for 0%

commit v1 on v0

--- a/solution.py
+++ b/solution.py
@@ -32,6 +32,12 @@
     up_scale,
     down_scale,
 ):
+
+    def _cover_surface(axis_k, d_out, page):
+        v1 = jnp.split(page, jax.lax.axis_size("tensor"), axis=d_out)
+        latest = jnp.stack(v1, axis=0)
+        return jnp.concatenate(jax.lax.all_to_all(latest, "tensor", 0, 0), axis=axis_k)
+
     groups = lax.axis_size("expert")
     local_tokens, feat_width = tokens.shape
     probs, chosen, per_expert, member = gate_tables(expert_ids, route_logits, groups)
@@ -55,7 +61,7 @@
     gate_all, up_all, down_all = (
         lax.all_to_all(w_gate, "tensor", split_axis=2, concat_axis=1, tiled=True),
         lax.all_to_all(w_up, "tensor", split_axis=2, concat_axis=1, tiled=True),
-        lax.all_to_all(w_down, "tensor", split_axis=2, concat_axis=1, tiled=True),
+        _cover_surface(1, 2, page=w_down),
     )
     gate_w = gate_all[0]
     up_w = up_all[0]

time: 1180 us -> 1060 us (0.90)
  other arithmetic: 385 us -> 259 us
  waiting for transfers between devices: 236 us -> 332 us
  local copies, waits for them, and re-layouts: 342 us -> 251 us
    all_to_all x1, waiting for transfers between devices: 0.01 us -> 142 us  [body(): lax.all_to_all(w_up, 'tensor', split_axis=2, concat_axis=1, tiled=True)]
    unnamed x5 -> x3, other arithmetic: 380 us -> 254 us
    unnamed x49 -> x48, local copies, waits for them, and re-layouts: 292 us -> 215 us
    all_to_all x1, waiting for transfers between devices: 63.9 us -> 18 us  [_cover_surface(): jax.lax.all_to_all(latest, 'tensor', 0, 0)]
    all_to_all x1 -> x0, local copies, waits for them, and re-layouts: 16.6 us -> none  [body(): lax.all_to_all(w_down, 'tensor', split_axis=2, concat_axis=1, tiled=True)]
  transfers between devices with their start and end apart: 10 -> 10, of which waited for: 6 -> 7; matrix products, arithmetic and copies ran while one was open for 65% -> 53% of each run, Pallas kernels for 0% -> 0%
where the time goes in v1:
time: 1060 us; the launch traced here: 1050 us
  waiting for transfers between devices  332 us (31%)
  other arithmetic  259 us (24%)
  local copies, waits for them, and re-layouts  251 us (24%)
  matrix products  129 us (12%)
  blocking collectives  35.3 us (3%)
  starting transfers between devices  32.4 us (3%)
  between operations  14.1 us (1%)
    unnamed x3, other arithmetic  254 us
    unnamed x48, local copies, waits for them, and re-layouts  215 us
    all_to_all x1, waiting for transfers between devices, body(): lax.all_to_all(w_up, 'tensor', split_axis=2, concat_axis=1, tiled=True)  142 us
    reduce_scatter x1, waiting for transfers between devices, body(): lax.psum_scatter(out_part.astype(jnp.bfloat16), 'tensor', scatter_dimensi...  61.4 us
    all_gather x1, waiting for transfers between devices, body(): lax.all_gather(got_grads.reshape(total_rows, feat_width), 'tensor', axis=...  43.5 us
    reduce_scatter x1, waiting for transfers between devices, body(): lax.psum_scatter(grad_part.astype(jnp.bfloat16), 'tensor', scatter_dimens...  38.8 us
    dot_general x3, matrix products, contract_rows(): lax.dot_general(left, right, (((0,), (0,)), ((), ())), preferred_element_...  34.2 us
    all_to_all x1, blocking collectives, body(): lax.all_to_all(send_grads, 'expert', split_axis=0, concat_axis=0, tiled=T...  23.4 us
  transfers between devices with their start and end apart: 10, of which 7 were waited for; matrix products, arithmetic and copies ran while one was open for 53% of the time, Pallas kernels for 0%

profile of v1, /device:TPU:0, one launch (start us, length us, event | category | flops | bytes accessed | tf_op | source)
XLA Modules:
  0.0 1052.7 jit_solution(350164132859021554)
XLA Ops:
  16.1 51.2 %copy.32 = bf16[1,768,8192]{1,0,2:T(2,128)(2,1)} copy(bf16[1,768,8192]{2,1,0:T(8,128)(2,1)} %param.14) | data formatting | bytes 25165824 | tf_op args[4]
  67.9 126.8 %reduce.1 = bf16[8192,768]{1,0:T(8,128)(2,1)} reduce(bf16[8192,1,768]{2,1,0:T(2,128)(2,1)} %bitcast.66, bf16[]{:T(256)} %broadcast.37), dimensions={1}, to_apply=%bitcast.46.reduce_sub_computation | reduce | bytes 25165826
  194.7 12.3 %reshape.42 = bf16[8,2,393216]{2,1,0:T(2,128)(2,1)} reshape(bf16[8192,768]{1,0:T(8,128)(2,1)} %reduce.1) | data formatting | bytes 25165824
  213.8 51.2 %copy.34 = bf16[1,768,8192]{1,0,2:T(2,128)(2,1)} copy(bf16[1,768,8192]{2,1,0:T(8,128)(2,1)} %param.15) | data formatting | bytes 25165824 | tf_op args[5]
  265.1 126.8 %reduce.2 = bf16[8192,768]{1,0:T(8,128)(2,1)} reduce(bf16[8192,1,768]{2,1,0:T(2,128)(2,1)} %bitcast.67, bf16[]{:T(256)} %broadcast.37), dimensions={1}, to_apply=%bitcast.44.reduce_sub_computation | reduce | bytes 25165826
  391.8 12.3 %reshape.40 = bf16[8,2,393216]{2,1,0:T(2,128)(2,1)} reshape(bf16[8192,768]{1,0:T(8,128)(2,1)} %reduce.2) | data formatting | bytes 25165824
  431.9 141.8 %all-to-all-done.2 = bf16[8,2,393216]{2,1,0:T(2,128)(2,1)} async-done(((bf16[8,2,393216]{2,1,0:T(2,128)(2,1)}), bf16[8,2,393216]{2,1,0:T(2,128)(2,1)}, u32[]{:S(2)}, u32[]{:S(2)}) %all-to-all-start.2) | async-done | bytes 12582944 | tf_op jit(solution)/shard_map/all_to_all | solution.py:63
  579.3 17.9 %reshape.43 = bf16[8192,1,768]{2,1,0:T(2,128)(2,1)} reshape(bf16[8,2,393216]{2,1,0:T(2,128)(2,1)} %all-to-all-done.1) | data formatting | bytes 25165824
  597.2 15.1 %copy.39 = bf16[1,768,8192]{1,2,0:T(8,128)(2,1)} copy(bf16[1,768,8192]{1,0,2:T(2,128)(2,1)} %bitcast.68) | data formatting | bytes 25165824
  612.3 16.6 %copy.33 = bf16[1,8,768,1024]{3,2,1,0:T(8,128)(2,1)} copy(bf16[1,8,768,1024]{2,3,1,0:T(8,128)(2,1)} %bitcast.70) | data formatting | bytes 25165824 | tf_op jit(solution)/shard_map/all_to_all | solution.py:62
  628.9 17.9 %reshape.41 = bf16[8192,1,768]{2,1,0:T(2,128)(2,1)} reshape(bf16[8,2,393216]{2,1,0:T(2,128)(2,1)} %all-to-all-done.2) | data formatting | bytes 25165824
  646.8 15.1 %copy.40 = bf16[1,768,8192]{1,2,0:T(8,128)(2,1)} copy(bf16[1,768,8192]{1,0,2:T(2,128)(2,1)} %bitcast.69) | data formatting | bytes 25165824
  661.9 16.6 %copy.35 = bf16[1,8,768,1024]{3,2,1,0:T(8,128)(2,1)} copy(bf16[1,8,768,1024]{2,3,1,0:T(8,128)(2,1)} %bitcast.71) | data formatting | bytes 25165824 | tf_op jit(solution)/shard_map/all_to_all | solution.py:63
  700.1 18.0 %all-to-all-done.3 = bf16[8,1,768,1024]{3,2,1,0:T(8,128)(2,1)} async-done(((bf16[8,1,768,1024]{3,2,1,0:T(8,128)(2,1)}), bf16[8,1,768,1024]{3,2,1,0:T(8,128)(2,1)}, u32[]{:S(2)}, u32[]{:S(2)}) %all-to-all-start.3) | async-done | bytes 12582944 | tf_op jit(solution)/shard_map/all_to_all | solution.py:39
  718.0 18.8 %convolution_convert_fusion = bf16[512,6144]{1,0:T(8,128)(2,1)} fusion(bf16[512,1024]{1,0:T(8,128)(2,1)S(1)} %get-tuple-element.14, bf16[6144,1024]{1,0:T(8,128)(2,1)} %bitcast.18), kind=kOutput, calls=%fused_computation.4 | convolution fusion | flops 6445596672 | bytes 19922944 | tf_op jit(solution)/shard_map/dot_general | solution.py:74
  736.9 61.4 %reduce-scatter.3.cloned.1.call-done = bf16[512,768]{1,0:T(8,128)(2,1)} async-done(((bf16[512,6144]{1,0:T(8,128)(2,1)}), bf16[512,768]{1,0:T(8,128)(2,1)}) %reduce-scatter.3.cloned.1.call-update) | async-done | bytes 786448 | tf_op jit(solution)/shard_map/reduce_scatter | solution.py:86
  802.9 19.9 %all-to-all-done.4 = bf16[4,128,768]{2,1,0:T(8,128)(2,1)S(1)} async-done(((bf16[4,128,768]{2,1,0:T(8,128)(2,1)}), bf16[4,128,768]{2,1,0:T(8,128)(2,1)S(1)}, u32[]{:S(2)}, u32[]{:S(2)}) %all-to-all-start.4) | async-done | bytes 786464 | tf_op jit(solution)/shard_map/all_to_all | solution.py:89
  836.9 23.4 %all_to_all.55 = bf16[4,128,768]{2,1,0:T(8,128)(2,1)} all-to-all(bf16[4,128,768]{2,1,0:T(8,128)(2,1)S(1)} %get-tuple-element.12), channel_id=1, replica_groups=mesh['expert'=4,'tensor'=8] {'expert'}, dimensions={0} | all-to-all | bytes 1572864 | tf_op jit(solution)/shard_map/all_to_all | solution.py:55
  860.3 43.5 %all-gather.5.cloned.1.call-done = bf16[512,6144]{1,0:T(8,128)(2,1)} async-done(((bf16[512,768]{1,0:T(8,128)(2,1)}), bf16[512,6144]{1,0:T(8,128)(2,1)}) %all-gather.5.cloned.1.call-update) | async-done | bytes 6291472 | tf_op jit(solution)/shard_map/all_gather | solution.py:59
  903.8 14.5 %multiply_convert_fusion = (bf16[512,1024]{1,0:T(8,128)(2,1)S(1)}, bf16[512,1024]{1,0:T(8,128)(2,1)S(1)}) fusion(f32[1024]{0:T(1024)S(1)} %bitcast.87, f32[1024]{0:T(1024)S(1)} %bitcast.89, f32[512,1024]{1,0:T(8,128)} %copy-done.13, f32[1024]{0:T(1024)S(1)} %bitcast.91, f32[512,1024]{1,0:T(8,128)} %get-tuple-element.15, ...), kind=kOutput, calls=%fused_computation.5 | convolution fusion | flops 6451888128 | bytes 25178112 | tf_op jit(solution)/shard_map/dot_general | solution.py:76
  918.4 20.2 %fusion.5 = f32[512,6144]{1,0:T(8,128)} fusion(bf16[512,1024]{1,0:T(8,128)(2,1)S(1)} %get-tuple-element.11, bf16[6144,1024]{1,0:T(8,128)(2,1)} %bitcast.73), kind=kOutput, calls=%fused_computation.35 | convolution fusion | flops 6442450944 | bytes 26214400 | tf_op jit(solution)/shard_map/dot_general | solution.py:83
  938.6 20.3 %add_convert_fusion = bf16[512,6144]{1,0:T(8,128)(2,1)} fusion(f32[512,6144]{1,0:T(8,128)} %fusion.5, bf16[512,1024]{1,0:T(8,128)(2,1)S(1)} %get-tuple-element.10, bf16[6144,1024]{1,0:T(8,128)(2,1)} %bitcast.74), kind=kOutput, calls=%fused_computation.3 | convolution fusion | flops 6448742400 | bytes 32505856 | tf_op jit(solution)/shard_map/dot_general | solution.py:83
  959.5 12.5 %convert_bitcast_fusion.1 = bf16[1,6144,1024]{2,1,0:T(8,128)(2,1)} fusion(bf16[512,6144]{1,0:T(8,128)(2,1)} %all-gather.3.cloned.1.call-done, bf16[512,1024]{1,0:T(8,128)(2,1)} %copy-done.12), kind=kOutput, calls=%fused_computation.1 | convolution fusion | flops 6448742400 | bytes 19922944 | tf_op jit(solution)/shard_map/dot_general | solution.py:18
  981.8 38.8 %reduce-scatter.5.cloned.1.call-done = bf16[512,768]{1,0:T(8,128)(2,1)} async-done(((bf16[512,6144]{1,0:T(8,128)(2,1)}), bf16[512,768]{1,0:T(8,128)(2,1)}) %reduce-scatter.5.cloned.1.call-update) | async-done | bytes 786448 | tf_op jit(solution)/shard_map/reduce_scatter | solution.py:96
  (77 shorter events, 125.8 us)
Async XLA Ops:
  9.8 197.2 %all-to-all-start = ((bf16[4,128,768]{2,1,0:T(8,128)(2,1)}), bf16[4,128,768]{2,1,0:T(8,128)(2,1)S(1)}, u32[]{:S(2)}, u32[]{:S(2)}) async-start(bf16[4,128,768]{2,1,0:T(8,128)(2,1)} %broadcast_multiply_fusion), calls=%async_computation | async-start | bytes 1572864 | tf_op jit(solution)/shard_map/all_to_all | solution.py:54
  207.9 196.3 %all-to-all-start.1 = ((bf16[8,2,393216]{2,1,0:T(2,128)(2,1)}), bf16[8,2,393216]{2,1,0:T(2,128)(2,1)}, u32[]{:S(2)}, u32[]{:S(2)}) async-start(bf16[8,2,393216]{2,1,0:T(2,128)(2,1)} %reshape.42), calls=%async_computation.1 | async-start | bytes 25165824 | tf_op jit(solution)/shard_map/all_to_all | solution.py:62
  404.1 169.6 %all-to-all-start.2 = ((bf16[8,2,393216]{2,1,0:T(2,128)(2,1)}), bf16[8,2,393216]{2,1,0:T(2,128)(2,1)}, u32[]{:S(2)}, u32[]{:S(2)}) async-start(bf16[8,2,393216]{2,1,0:T(2,128)(2,1)} %reshape.40), calls=%async_computation.2 | async-start | bytes 25165824 | tf_op jit(solution)/shard_map/all_to_all | solution.py:63
  409.5 269.0 %all-gather.3.cloned.1.call-start = ((), (), s32[]{:S(2)}) async-start(), calls=%async_computation.9 | async-start | bytes 7077888 | tf_op jit(solution)/shard_map/all_gather | solution.py:58
  573.7 144.3 %all-to-all-start.3 = ((bf16[8,1,768,1024]{3,2,1,0:T(8,128)(2,1)}), bf16[8,1,768,1024]{3,2,1,0:T(8,128)(2,1)}, u32[]{:S(2)}, u32[]{:S(2)}) async-start(bf16[8,1,768,1024]{3,2,1,0:T(8,128)(2,1)} %bitcast_dynamic-update-slice_fusion), calls=%async_computation.3 | async-start | bytes 25165824 | tf_op jit(solution)/shard_map/all_to_all | solution.py:39
  579.1 219.2 %reduce-scatter.3.cloned.1.call-start = ((), (), s32[]{:S(2)}) async-start(), calls=%async_computation.10 | async-start | bytes 7077888 | tf_op jit(solution)/shard_map/reduce_scatter | solution.py:86
  678.5 13.2 %copy-start = (bf16[1,8,768,1024]{3,2,1,0:T(8,128)(2,1)S(1)}, bf16[1,8,768,1024]{3,2,1,0:T(8,128)(2,1)}, u32[]{:S(2)}) copy-start(bf16[1,8,768,1024]{3,2,1,0:T(8,128)(2,1)} %copy.35) | copy-start | bytes 37748740
  678.5 13.2 %copy-start.5 = (bf16[512,6144]{1,0:T(8,128)(2,1)S(1)}, bf16[512,6144]{1,0:T(8,128)(2,1)}, u32[]{:S(2)}) copy-start(bf16[512,6144]{1,0:T(8,128)(2,1)} %all-gather.3.cloned.1.call-done) | copy-start | bytes 18874372
  678.5 13.2 %copy-start.6 = (f32[1,1024]{1,0:T(1,128)S(1)}, f32[1,1024]{1,0:T(1,128)}, u32[]{:S(2)}) copy-start(f32[1,1024]{1,0:T(1,128)} %param.19) | copy-start | bytes 12292
  678.5 13.2 %copy-start.7 = (f32[1,1024]{1,0:T(1,128)S(1)}, f32[1,1024]{1,0:T(1,128)}, u32[]{:S(2)}) copy-start(f32[1,1024]{1,0:T(1,128)} %param.18) | copy-start | bytes 12292
  678.5 13.2 %copy-start.8 = (f32[1,1024]{1,0:T(1,128)S(1)}, f32[1,1024]{1,0:T(1,128)}, u32[]{:S(2)}) copy-start(f32[1,1024]{1,0:T(1,128)} %param.17) | copy-start | bytes 12292
  700.1 36.8 %copy-start.11 = (bf16[512,1024]{1,0:T(8,128)(2,1)}, bf16[512,1024]{1,0:T(8,128)(2,1)S(1)}, u32[]{:S(2)}) copy-start(bf16[512,1024]{1,0:T(8,128)(2,1)S(1)} %get-tuple-element.14) | copy-start | bytes 3145732
  718.0 84.8 %copy-start.2 = (bf16[128,768]{1,0:T(8,128)(2,1)S(1)}, bf16[128,768]{1,0:T(8,128)(2,1)}, u32[]{:S(2)}) copy-start(bf16[128,768]{1,0:T(8,128)(2,1)} %param.11) | copy-start | bytes 589828
  718.0 84.9 %copy-start.4 = (f32[128,2]{0,1:T(2,128)S(1)}, f32[128,2]{0,1:T(2,128)}, u32[]{:S(2)}) copy-start(f32[128,2]{0,1:T(2,128)} %param.13) | copy-start | bytes 3076
  736.9 99.0 %copy-start.3 = (s32[128,2]{0,1:T(2,128)S(1)}, s32[128,2]{0,1:T(2,128)}, u32[]{:S(2)}) copy-start(s32[128,2]{0,1:T(2,128)} %param.12) | copy-start | bytes 3076
  798.3 24.5 %all-to-all-start.4 = ((bf16[4,128,768]{2,1,0:T(8,128)(2,1)}), bf16[4,128,768]{2,1,0:T(8,128)(2,1)S(1)}, u32[]{:S(2)}, u32[]{:S(2)}) async-start(bf16[4,128,768]{2,1,0:T(8,128)(2,1)} %bitcast.79), calls=%async_computation.5 | async-start | bytes 1572864 | tf_op jit(solution)/shard_map/all_to_all | solution.py:89
  802.9 100.9 %all-gather.5.cloned.1.call-start = ((), (), s32[]{:S(2)}) async-start(), calls=%async_computation.11 | async-start | bytes 7077888 | tf_op jit(solution)/shard_map/all_gather | solution.py:59
  860.3 160.3 %reduce-scatter.5.cloned.1.call-start = ((), (), s32[]{:S(2)}) async-start(), calls=%async_computation.12 | async-start | bytes 7077888 | tf_op jit(solution)/shard_map/reduce_scatter | solution.py:96
  918.3 20.2 %copy-start.9 = (bf16[512,1024]{1,0:T(8,128)(2,1)}, bf16[512,1024]{1,0:T(8,128)(2,1)S(1)}, u32[]{:S(2)}) copy-start(bf16[512,1024]{1,0:T(8,128)(2,1)S(1)} %get-tuple-element.11) | copy-start | bytes 3145732
  918.4 20.2 %copy-start.12 = (bf16[512,1024]{1,0:T(8,128)(2,1)}, bf16[512,1024]{1,0:T(8,128)(2,1)S(1)}, u32[]{:S(2)}) copy-start(bf16[512,1024]{1,0:T(8,128)(2,1)S(1)} %get-tuple-element.10) | copy-start | bytes 3145732
  958.8 13.2 %slice-start = ((s8[6291456]{0:T(1024)(128)(4,1)}), s8[2097152]{0:T(1024)(128)(4,1)S(1)}, s32[]{:S(2)}) async-start(s8[6291456]{0:T(1024)(128)(4,1)} %bitcast.84), calls=%async_computation.13 | async-start | bytes 4194304
  959.5 12.5 %slice-start.1 = ((s8[6291456]{0:T(1024)(128)(4,1)}), s8[4194304]{0:T(1024)(128)(4,1)S(1)}, s32[]{:S(2)}) async-start(s8[6291456]{0:T(1024)(128)(4,1)} %bitcast.84), calls=%async_computation.14 | async-start | bytes 8388608
  959.5 12.5 %copy-start.10 = (bf16[512,1024]{1,0:T(8,128)(2,1)S(1)}, bf16[512,1024]{1,0:T(8,128)(2,1)}, u32[]{:S(2)}) copy-start(bf16[512,1024]{1,0:T(8,128)(2,1)} %copy-done.9) | copy-start | bytes 3145732
  1020.6 24.5 %all-to-all-start.6 = ((bf16[4,128,768]{2,1,0:T(8,128)(2,1)}), bf16[4,128,768]{2,1,0:T(8,128)(2,1)S(1)}, u32[]{:S(2)}, u32[]{:S(2)}) async-start(bf16[4,128,768]{2,1,0:T(8,128)(2,1)} %bitcast.78), calls=%async_computation.8 | async-start | bytes 1572864 | tf_op jit(solution)/shard_map/all_to_all | solution.py:99
  (2 other events, 2.2 us)
Sparse Core Ops, SparseCore 0:
  412.2 112.5 all-gather.2
  737.0 61.2 reduce-scatter.2
  860.4 43.3 all-gather.4
  959.0 61.5 reduce-scatter.4
